TPU v7x, 512 devices: a whole 4x4x16 slice. The times are simulated.
512 devices in a mesh: cuts: 128 (over z, x, core), stem: 4 (over y).
Axes of the slice: x: 4, y: 4, z: 16, core: 2. Of those that a mesh axis runs over, the one named last changes fastest.
Arguments:
- stem_tensor: bfloat16 [8, 64, 1024], P('stem'), may hold values from -6 to 6
- mid_tensors: bfloat16 [8192, 512, 128], P(('cuts', 'stem')), may hold values from -0.1875 to 0.1875
- right_tensors: bfloat16 [8, 8192, 64, 128], P(None, ('cuts', 'stem')), may hold values from -0.001953125 to 0.001953125
Outputs:
- amplitudes: float32 [8192], P('cuts')
All inputs are finite; a program needn't handle non-finite values.
Results may differ from a plain program's by a relative error of at most 0.0029.
Values may be sent and summed in bfloat16 or wider, within the bound.
A program may use at most 64 MiB of HBM per device.

v0:
```python
import jax
import jax.numpy as jnp
from jax import lax
from jax.sharding import PartitionSpec as P


def widen(tensor):
    half_width = tensor.shape[-1] // 2
    real_part = tensor[..., :half_width]
    imag_part = tensor[..., half_width:]
    upper_rows = jnp.concatenate([real_part, imag_part], axis=-1)
    lower_rows = jnp.concatenate([-imag_part, real_part], axis=-1)
    return jnp.concatenate([upper_rows, lower_rows], axis=-2)


def on_device(stem_tensor, mid_tensors, right_tensors):
    local_blocks, rows_a, width = stem_tensor.shape
    cols_b = right_tensors.shape[-1]
    widened = jnp.moveaxis(widen(mid_tensors), 0, 1).reshape(width, -1)
    fragment = lax.all_gather(stem_tensor, "stem", axis=0, tiled=True)
    flattened = fragment.reshape(-1, width)
    product = jnp.dot(flattened, widened, preferred_element_type=jnp.float32)
    first_step = product.astype(jnp.bfloat16).reshape(fragment.shape[0], rows_a, -1)
    right_wide = widen(right_tensors).reshape(first_step.shape[0], -1, cols_b)
    partial_sum = jnp.einsum(
        "iaq,iqb->ab", first_step, right_wide, preferred_element_type=jnp.float32
    ).reshape(-1)
    summed = lax.psum(partial_sum, ("cuts", "stem"))
    portion = partial_sum.shape[0] // lax.axis_size("cuts")
    return lax.dynamic_slice_in_dim(summed, lax.axis_index("cuts") * portion, portion)


def solution(mesh):
    return jax.shard_map(
        on_device,
        mesh=mesh,
        in_specs=(
            P("stem", None, None),
            P(("cuts", "stem"), None, None),
            P(None, ("cuts", "stem"), None, None),
        ),
        out_specs=P("cuts"),
        check_vma=False,
    )
```

profile of v0, /device:TPU:1, one launch (start us, length us, event | category | flops | bytes accessed | tf_op | source)
XLA Modules:
  0.0 163.8 jit_solution(10493150595197969950)
XLA Ops:
  6.5 0.0 all-gather.2.cloned.1.call-start
  6.5 0.7 all-gather.2.cloned.1.call-update
  7.3 2.9 %copy.9 = bf16[16,512,128]{1,2,0:T(8,128)(2,1)S(1)} copy(bf16[16,512,128]{2,1,0:T(8,128)(2,1)} %param.4) | data formatting | bytes 4194304 | tf_op args[1]
  10.1 0.1 slice_negate_fusion.1
  10.3 0.0 copy-start.1
  10.3 2.2 %maximum_maximum_fusion = bf16[16,1024,128]{1,2,0:T(8,128)(2,1)} fusion(bf16[16,512,64]{1,2,0:T(8,128)(2,1)S(1)} %get-tuple-element.8, bf16[16,512,64]{1,2,0:T(8,128)(2,1)S(1)} %get-tuple-element.7, bf16[16,512,128]{1,2,0:T(8,128)(2,1)S(1)} %copy.9), kind=kLoop, calls=%fused_computation | loop fusion | flops 12582912 | bytes 8388608 | tf_op jit(solution)/shard_map/concatenate | solution.py:13
  12.5 0.1 copy-done.1
  12.6 0.9 slice_negate_fusion
  13.5 3.5 %maximum_maximum_fusion.1 = bf16[8,16,128,128]{3,2,1,0:T(8,128)(2,1)} fusion(bf16[8,16,64,64]{3,2,1,0:T(8,128)(2,1)S(1)} %get-tuple-element.6, bf16[8,16,64,64]{3,2,1,0:T(8,128)(2,1)S(1)} %get-tuple-element.5, bf16[8,16,64,128]{3,2,1,0:T(8,128)(2,1)S(1)} %copy-done.1), kind=kLoop, calls=%fused_computation.1 | loop fusion | flops 12582912 | bytes 8388608 | tf_op jit(solution)/shard_map/concatenate | solution.py:13
  17.0 28.6 %all-gather.2.cloned.1.call-done = bf16[8,64,1024]{2,1,0:T(8,128)(2,1)} async-done(((bf16[2,64,1024]{2,1,0:T(8,128)(2,1)}), bf16[8,64,1024]{2,1,0:T(8,128)(2,1)}) %all-gather.2.cloned.1.call-update) | async-done | bytes 1048592 | tf_op jit(solution)/shard_map/all_gather | solution.py:20
  45.6 0.0 copy-start
  45.6 5.0 %convolution_convert_fusion = bf16[2048,512]{0,1:T(8,128)(2,1)S(1)} fusion(bf16[1024,2048]{0,1:T(8,128)(2,1)} %bitcast.18, bf16[512,1024]{1,0:T(8,128)(2,1)} %bitcast.19), kind=kOutput, calls=%fused_computation.2 | convolution fusion | flops 2148532224 | bytes 7340032 | tf_op jit(solution)/shard_map/dot_general | solution.py:22
  50.6 0.0 copy-done
  50.6 0.9 convolution_bitcast_fusion
  51.4 105.0 %psum.7 = f32[8192]{0:T(1024)S(1)} all-reduce(f32[8192]{0:T(1024)S(1)} %convolution_bitcast_fusion), channel_id=1, replica_groups=mesh['cuts'=128,'stem'=4] {'cuts','stem'}, use_global_device_ids=true, to_apply=%region_0.0 | all-reduce | flops 8192 | bytes 65536 | tf_op jit(solution)/shard_map/psum | solution.py:28
  156.4 0.6 dynamic_slice.3
Async XLA Ops:
  6.5 39.0 %all-gather.2.cloned.1.call-start = ((), (), s32[]{:S(2)}) async-start(), calls=%async_computation | async-start | bytes 1310720 | tf_op jit(solution)/shard_map/all_gather | solution.py:20
  10.3 2.3 %copy-start.1 = (bf16[8,16,64,128]{3,2,1,0:T(8,128)(2,1)S(1)}, bf16[8,16,64,128]{3,2,1,0:T(8,128)(2,1)}, u32[]{:S(2)}) copy-start(bf16[8,16,64,128]{3,2,1,0:T(8,128)(2,1)} %param.5) | copy-start | bytes 6291460
  45.6 5.0 %copy-start = (bf16[8,16,128,128]{3,2,1,0:T(8,128)(2,1)S(1)}, bf16[8,16,128,128]{3,2,1,0:T(8,128)(2,1)}, u32[]{:S(2)}) copy-start(bf16[8,16,128,128]{3,2,1,0:T(8,128)(2,1)} %maximum_maximum_fusion.1) | copy-start | bytes 12582916
Sparse Core Ops, SparseCore 0:
  9.5 36.0 all-gather.1
where the time goes:
time: 164 us
  blocking collectives  105 us (64%)
  waiting for transfers between devices  29.3 us (18%)
  between operations  13.4 us (8%)
  other arithmetic  6.78 us (4%)
  matrix products  5.86 us (4%)
  local copies, waits for them, and re-layouts  3.52 us (2%)
    psum x1, blocking collectives, on_device(): summed = lax.psum(partial_sum, ('cuts', 'stem'))  105 us
    all_gather x1, waiting for transfers between devices, on_device(): fragment = lax.all_gather(stem_tensor, 'stem', axis=0, tiled=True)  28.6 us
    concatenate x2, other arithmetic, widen(): return jnp.concatenate([upper_rows, lower_rows], axis=-2)  5.77 us
    dot_general x1, matrix products, on_device(): product = jnp.dot(flattened, widened, preferred_element_type=jnp.float32)  5.01 us
  transfers between devices with their start and end apart: 1, of which 1 were waited for; matrix products, arithmetic and copies ran while one was open for 6% of the time, Pallas kernels for 0%

commit v1 on v0

--- a/solution.py
+++ b/solution.py
@@ -17,7 +17,12 @@
     local_blocks, rows_a, width = stem_tensor.shape
     cols_b = right_tensors.shape[-1]
     widened = jnp.moveaxis(widen(mid_tensors), 0, 1).reshape(width, -1)
-    fragment = lax.all_gather(stem_tensor, "stem", axis=0, tiled=True)
+    ring = [stem_tensor]
+    for hop in range(3):
+        ring.append(lax.ppermute(ring[-1], "stem", [(dev, (dev + 1) % 4) for dev in range(4)]))
+    fragment = jnp.roll(
+        jnp.concatenate(ring[::-1], axis=0), (lax.axis_index("stem") + 1) * ring[0].shape[0], axis=0
+    )
     flattened = fragment.reshape(-1, width)
     product = jnp.dot(flattened, widened, preferred_element_type=jnp.float32)
     first_step = product.astype(jnp.bfloat16).reshape(fragment.shape[0], rows_a, -1)

time: 164 us -> 147 us (0.90)
  waiting for transfers between devices: 29.3 us -> 8.04 us
  between operations: 13.4 us -> 0.22 us
  starting transfers between devices: 0.01 us -> 9.65 us
  blocking collectives: 105 us -> 113 us
  matrix products: 5.86 us -> 3.23 us
    all_gather x1 -> x0, waiting for transfers between devices: 28.6 us -> none  [on_device(): fragment = lax.all_gather(stem_tensor, 'stem', axis=0, tiled=True)]
    ppermute x0 -> x3, starting transfers between devices: none -> 9.65 us  [on_device(): lax.ppermute(ring[-1], 'stem', [(dev, (dev + 1) % 4) for dev in range(4)])]
    ppermute x0 -> x3, waiting for transfers between devices: none -> 8.04 us  [on_device(): lax.ppermute(ring[-1], 'stem', [(dev, (dev + 1) % 4) for dev in range(4)])]
    psum x1, blocking collectives: 105 us -> 113 us  [on_device(): summed = lax.psum(partial_sum, ('cuts', 'stem'))]
    neg x2, other arithmetic: 1.01 us -> 4.71 us  [widen(): lower_rows = jnp.concatenate([-imag_part, real_part], axis=-1)]
    concatenate x2, other arithmetic: 5.77 us -> 2.89 us  [widen(): return jnp.concatenate([upper_rows, lower_rows], axis=-2)]
    dot_general x1, matrix products: 5.01 us -> 2.38 us  [on_device(): product = jnp.dot(flattened, widened, preferred_element_type=jnp.float32)]
    unnamed x5 -> x18, local copies, waits for them, and re-layouts: 2.94 us -> 4.22 us
  transfers between devices with their start and end apart: 1 -> 3, of which waited for: 1 -> 2; matrix products, arithmetic and copies ran while one was open for 6% -> 8% of each run, Pallas kernels for 0% -> 0%
where the time goes in v1:
time: 147 us; the launch traced here: 146 us
  blocking collectives  113 us (77%)
  starting transfers between devices  9.65 us (7%)
  waiting for transfers between devices  8.04 us (5%)
  other arithmetic  7.6 us (5%)
  local copies, waits for them, and re-layouts  4.9 us (3%)
  matrix products  3.23 us (2%)
    psum x1, blocking collectives, on_device(): summed = lax.psum(partial_sum, ('cuts', 'stem'))  113 us
    ppermute x3, starting transfers between devices, on_device(): lax.ppermute(ring[-1], 'stem', [(dev, (dev + 1) % 4) for dev in range(4)])  9.65 us
    ppermute x3, waiting for transfers between devices, on_device(): lax.ppermute(ring[-1], 'stem', [(dev, (dev + 1) % 4) for dev in range(4)])  8.04 us
    neg x2, other arithmetic, widen(): lower_rows = jnp.concatenate([-imag_part, real_part], axis=-1)  4.71 us
    unnamed x18, local copies, waits for them, and re-layouts  4.22 us
  transfers between devices with their start and end apart: 3, of which 2 were waited for; matrix products, arithmetic and copies ran while one was open for 8% of the time, Pallas kernels for 0%

profile of v1, /device:TPU:1, one launch (start us, length us, event | category | flops | bytes accessed | tf_op | source)
XLA Modules:
  0.0 146.2 jit_solution(10508278838340089739)
XLA Ops:
  0.0 4.0 %collective-permute-start = (bf16[2,64,1024]{2,1,0:T(8,128)(2,1)}, bf16[2,64,1024]{2,1,0:T(8,128)(2,1)S(1)}, u32[]{:S(2)}, u32[]{:S(2)}) collective-permute-start(bf16[2,64,1024]{2,1,0:T(8,128)(2,1)} %param.3), channel_id=1, source_target_pairs={{0,1},{1,2},{2,3},{3,0},{4,5},{5,6},{6,7},{7,4},{8,9},{9,10},{10,1... | collective-permute-start | bytes 786440 | tf_op jit(solution)/shard_map/ppermute | solution.py:22
  4.1 0.0 copy-start
  4.1 4.1 %copy.6 = bf16[16,512,128]{1,2,0:T(8,128)(2,1)} copy(bf16[16,512,128]{2,1,0:T(8,128)(2,1)} %param.4) | data formatting | bytes 4194304 | tf_op args[1]
  8.1 0.0 copy-done
  8.1 2.9 %slice_negate_fusion = (bf16[8,16,64,64]{3,2,1,0:T(8,128)(2,1)}, bf16[8,16,64,64]{3,2,1,0:T(8,128)(2,1)}) fusion(bf16[8,16,64,128]{3,2,1,0:T(8,128)(2,1)S(1)} %copy-done), kind=kLoop, calls=%fused_computation.3 | loop fusion | flops 524288 | bytes 4194304 | tf_op jit(solution)/shard_map/neg | solution.py:12
  11.0 0.0 copy-start.1
  11.0 1.8 %slice_negate_fusion.1 = (bf16[16,512,64]{1,2,0:T(8,128)(2,1)S(1)}, bf16[16,512,64]{1,2,0:T(8,128)(2,1)S(1)}) fusion(bf16[16,512,128]{1,2,0:T(8,128)(2,1)} %copy.6), kind=kLoop, calls=%fused_computation.5 | loop fusion | flops 524288 | bytes 4194304 | tf_op jit(solution)/shard_map/neg | solution.py:12
  12.8 0.0 collective-permute-done
  12.9 3.2 %collective-permute-start.1 = (bf16[2,64,1024]{2,1,0:T(8,128)(2,1)S(1)}, bf16[2,64,1024]{2,1,0:T(8,128)(2,1)S(1)}, u32[]{:S(2)}, u32[]{:S(2)}) collective-permute-start(bf16[2,64,1024]{2,1,0:T(8,128)(2,1)S(1)} %collective-permute-done), channel_id=1, source_target_pairs={{0,1},{1,2},{2,3},{3,0},{4,5},{5,6},{6,7},{7,4},{8,9},{9,10},{10,1... | collective-permute-start | bytes 786440 | tf_op jit(solution)/shard_map/ppermute | solution.py:22
  16.1 0.0 copy-done.1
  16.1 0.0 copy-start.2
  16.1 0.0 copy-start.3
  16.1 0.6 maximum_maximum_fusion
  16.7 4.5 %collective-permute-done.1 = bf16[2,64,1024]{2,1,0:T(8,128)(2,1)S(1)} collective-permute-done((bf16[2,64,1024]{2,1,0:T(8,128)(2,1)S(1)}, bf16[2,64,1024]{2,1,0:T(8,128)(2,1)S(1)}, u32[]{:S(2)}, u32[]{:S(2)}) %collective-permute-start.1) | collective-permute-done | bytes 262176 | tf_op jit(solution)/shard_map/ppermute | solution.py:22
  21.2 2.4 %collective-permute-start.2 = (bf16[2,64,1024]{2,1,0:T(8,128)(2,1)S(1)}, bf16[2,64,1024]{2,1,0:T(8,128)(2,1)S(1)}, u32[]{:S(2)}, u32[]{:S(2)}) collective-permute-start(bf16[2,64,1024]{2,1,0:T(8,128)(2,1)S(1)} %collective-permute-done.1), channel_id=1, source_target_pairs={{0,1},{1,2},{2,3},{3,0},{4,5},{5,6},{6,7},{7,4},{8,9},{9,10},{10,1... | collective-permute-start | bytes 786440 | tf_op jit(solution)/shard_map/ppermute | solution.py:22
  23.6 0.0 copy-done.2
  23.6 0.0 copy-done.3
  23.6 0.0 copy-start.4
  23.6 2.3 %maximum_maximum_fusion.1 = bf16[8,16,128,128]{3,2,1,0:T(8,128)(2,1)S(1)} fusion(bf16[8,16,64,64]{3,2,1,0:T(8,128)(2,1)S(1)} %copy-done.3, bf16[8,16,64,64]{3,2,1,0:T(8,128)(2,1)S(1)} %copy-done.2, bf16[8,16,64,128]{3,2,1,0:T(8,128)(2,1)S(1)} %copy-done), kind=kLoop, calls=%fused_computation.1 | loop fusion | flops 12582912 | bytes 8388608 | tf_op jit(solution)/shard_map/concatenate | solution.py:13
  26.0 3.5 %collective-permute-done.2 = bf16[2,64,1024]{2,1,0:T(8,128)(2,1)S(1)} collective-permute-done((bf16[2,64,1024]{2,1,0:T(8,128)(2,1)S(1)}, bf16[2,64,1024]{2,1,0:T(8,128)(2,1)S(1)}, u32[]{:S(2)}, u32[]{:S(2)}) %collective-permute-start.2) | collective-permute-done | bytes 262176 | tf_op jit(solution)/shard_map/ppermute | solution.py:22
  29.6 0.0 copy-done.4
  29.7 0.1 constant_dynamic-slice_fusion
  29.8 2.4 %convolution_convert_fusion = bf16[512,2048]{1,0:T(8,128)(2,1)S(1)} fusion(bf16[512,1024]{1,0:T(8,128)(2,1)S(1)} %bitcast.17, bf16[1024,2048]{0,1:T(8,128)(2,1)S(1)} %bitcast.16), kind=kOutput, calls=%fused_computation.2 | convolution fusion | flops 2148532224 | bytes 7340032 | tf_op jit(solution)/shard_map/dot_general | solution.py:27
  32.2 0.9 convolution_bitcast_fusion
  33.1 112.6 %psum.7 = f32[8192]{0:T(1024)S(1)} all-reduce(f32[8192]{0:T(1024)S(1)} %convolution_bitcast_fusion), channel_id=1, replica_groups=mesh['cuts'=128,'stem'=4] {'cuts','stem'}, use_global_device_ids=true, to_apply=%region_0.1 | all-reduce | flops 8192 | bytes 65536 | tf_op jit(solution)/shard_map/psum | solution.py:33
  145.7 0.6 dynamic_slice.8
  (8 shorter events, 0.2 us)
Async XLA Ops:
  0.0 12.9 %collective-permute-start = (bf16[2,64,1024]{2,1,0:T(8,128)(2,1)}, bf16[2,64,1024]{2,1,0:T(8,128)(2,1)S(1)}, u32[]{:S(2)}, u32[]{:S(2)}) collective-permute-start(bf16[2,64,1024]{2,1,0:T(8,128)(2,1)} %param.3), channel_id=1, source_target_pairs={{0,1},{1,2},{2,3},{3,0},{4,5},{5,6},{6,7},{7,4},{8,9},{9,10},{10,1... | collective-permute-start | bytes 786440 | tf_op jit(solution)/shard_map/ppermute | solution.py:22
  4.1 4.1 %copy-start = (bf16[8,16,64,128]{3,2,1,0:T(8,128)(2,1)S(1)}, bf16[8,16,64,128]{3,2,1,0:T(8,128)(2,1)}, u32[]{:S(2)}) copy-start(bf16[8,16,64,128]{3,2,1,0:T(8,128)(2,1)} %param.5) | copy-start | bytes 6291460
  11.0 5.1 %copy-start.1 = (bf16[16,512,128]{1,2,0:T(8,128)(2,1)S(1)}, bf16[16,512,128]{1,2,0:T(8,128)(2,1)}, u32[]{:S(2)}) copy-start(bf16[16,512,128]{1,2,0:T(8,128)(2,1)} %copy.6) | copy-start | bytes 6291460
  12.9 8.3 %collective-permute-start.1 = (bf16[2,64,1024]{2,1,0:T(8,128)(2,1)S(1)}, bf16[2,64,1024]{2,1,0:T(8,128)(2,1)S(1)}, u32[]{:S(2)}, u32[]{:S(2)}) collective-permute-start(bf16[2,64,1024]{2,1,0:T(8,128)(2,1)S(1)} %collective-permute-done), channel_id=1, source_target_pairs={{0,1},{1,2},{2,3},{3,0},{4,5},{5,6},{6,7},{7,4},{8,9},{9,10},{10,1... | collective-permute-start | bytes 786440 | tf_op jit(solution)/shard_map/ppermute | solution.py:22
  16.1 7.5 %copy-start.2 = (bf16[8,16,64,64]{3,2,1,0:T(8,128)(2,1)S(1)}, bf16[8,16,64,64]{3,2,1,0:T(8,128)(2,1)}, u32[]{:S(2)}) copy-start(bf16[8,16,64,64]{3,2,1,0:T(8,128)(2,1)} %get-tuple-element.5) | copy-start | bytes 3145732
  16.1 7.5 %copy-start.3 = (bf16[8,16,64,64]{3,2,1,0:T(8,128)(2,1)S(1)}, bf16[8,16,64,64]{3,2,1,0:T(8,128)(2,1)}, u32[]{:S(2)}) copy-start(bf16[8,16,64,64]{3,2,1,0:T(8,128)(2,1)} %get-tuple-element.6) | copy-start | bytes 3145732
  21.2 8.3 %collective-permute-start.2 = (bf16[2,64,1024]{2,1,0:T(8,128)(2,1)S(1)}, bf16[2,64,1024]{2,1,0:T(8,128)(2,1)S(1)}, u32[]{:S(2)}, u32[]{:S(2)}) collective-permute-start(bf16[2,64,1024]{2,1,0:T(8,128)(2,1)S(1)} %collective-permute-done.1), channel_id=1, source_target_pairs={{0,1},{1,2},{2,3},{3,0},{4,5},{5,6},{6,7},{7,4},{8,9},{9,10},{10,1... | collective-permute-start | bytes 786440 | tf_op jit(solution)/shard_map/ppermute | solution.py:22
  23.6 5.9 %copy-start.4 = (bf16[2,64,1024]{2,1,0:T(8,128)(2,1)S(1)}, bf16[2,64,1024]{2,1,0:T(8,128)(2,1)}, u32[]{:S(2)}) copy-start(bf16[2,64,1024]{2,1,0:T(8,128)(2,1)} %param.3) | copy-start | bytes 786436

commit v2 on v0

--- a/solution.py
+++ b/solution.py
@@ -25,7 +25,7 @@
     partial_sum = jnp.einsum(
         "iaq,iqb->ab", first_step, right_wide, preferred_element_type=jnp.float32
     ).reshape(-1)
-    summed = lax.psum(partial_sum, ("cuts", "stem"))
+    summed = lax.psum(lax.psum(partial_sum, "stem"), "cuts")
     portion = partial_sum.shape[0] // lax.axis_size("cuts")
     return lax.dynamic_slice_in_dim(summed, lax.axis_index("cuts") * portion, portion)
 

time: 164 us -> 566 us (3.45)
  blocking collectives: 105 us -> 504 us
    psum x1 -> x2, blocking collectives: 105 us -> 504 us  [on_device(): summed = lax.psum(lax.psum(partial_sum, 'stem'), 'cuts')]
  transfers between devices with their start and end apart: 1 -> 1, of which waited for: 1 -> 1; matrix products, arithmetic and copies ran while one was open for 6% -> 2% of each run, Pallas kernels for 0% -> 0%
where the time goes in v2:
time: 566 us; the launch traced here: 563 us
  blocking collectives  504 us (89%)
  waiting for transfers between devices  29.3 us (5%)
  between operations  13.5 us (2%)
  other arithmetic  6.77 us (1%)
  matrix products  5.86 us (1%)
    psum x2, blocking collectives, on_device(): summed = lax.psum(lax.psum(partial_sum, 'stem'), 'cuts')  504 us
    all_gather x1, waiting for transfers between devices, on_device(): fragment = lax.all_gather(stem_tensor, 'stem', axis=0, tiled=True)  28.6 us
  transfers between devices with their start and end apart: 1, of which 1 were waited for; matrix products, arithmetic and copies ran while one was open for 2% of the time, Pallas kernels for 0%

profile of v2, /device:TPU:1, one launch (start us, length us, event | category | flops | bytes accessed | tf_op | source)
XLA Modules:
  0.0 563.0 jit_solution(8073140125641395160)
XLA Ops:
  6.5 0.0 all-gather.2.cloned.1.call-start
  6.5 0.7 all-gather.2.cloned.1.call-update
  7.3 2.9 copy.9
  10.1 0.1 slice_negate_fusion.1
  10.3 0.0 copy-start.1
  10.3 2.2 maximum_maximum_fusion
  12.5 0.1 copy-done.1
  12.6 0.9 slice_negate_fusion
  13.5 3.5 maximum_maximum_fusion.1
  17.0 28.6 %all-gather.2.cloned.1.call-done = bf16[8,64,1024]{2,1,0:T(8,128)(2,1)} async-done(((bf16[2,64,1024]{2,1,0:T(8,128)(2,1)}), bf16[8,64,1024]{2,1,0:T(8,128)(2,1)}) %all-gather.2.cloned.1.call-update) | async-done | bytes 1048592 | tf_op jit(solution)/shard_map/all_gather | solution.py:20
  45.6 0.0 copy-start
  45.6 5.0 convolution_convert_fusion
  50.6 0.0 copy-done
  50.6 0.9 convolution_bitcast_fusion
  51.4 12.1 %psum.14 = f32[8192]{0:T(1024)S(1)} all-reduce(f32[8192]{0:T(1024)S(1)} %convolution_bitcast_fusion), channel_id=1, replica_groups=mesh['cuts'=128,'stem'=4] {'stem'}, use_global_device_ids=true, to_apply=%region_0.0 | all-reduce | flops 8192 | bytes 65536 | tf_op jit(solution)/shard_map/psum | solution.py:28
  63.6 492.0 %psum.15 = f32[8192]{0:T(1024)S(1)} all-reduce(f32[8192]{0:T(1024)S(1)} %psum.14), channel_id=1, replica_groups=mesh['cuts'=128,'stem'=4] {'cuts'}, use_global_device_ids=true, to_apply=%region_1.0 | all-reduce | flops 8192 | bytes 65536 | tf_op jit(solution)/shard_map/psum | solution.py:28
  555.5 0.6 dynamic_slice.3
Async XLA Ops:
  6.5 39.0 %all-gather.2.cloned.1.call-start = ((), (), s32[]{:S(2)}) async-start(), calls=%async_computation | async-start | bytes 1310720 | tf_op jit(solution)/shard_map/all_gather | solution.py:20
  10.3 2.3 copy-start.1
  45.6 5.0 copy-start
Sparse Core Ops, SparseCore 0:
  9.5 36.0 all-gather.1

commit v3 on v0

--- a/solution.py
+++ b/solution.py
@@ -25,7 +25,7 @@
     partial_sum = jnp.einsum(
         "iaq,iqb->ab", first_step, right_wide, preferred_element_type=jnp.float32
     ).reshape(-1)
-    summed = lax.psum(partial_sum, ("cuts", "stem"))
+    summed = jnp.sum(lax.all_gather(partial_sum, ("cuts", "stem")), axis=0)
     portion = partial_sum.shape[0] // lax.axis_size("cuts")
     return lax.dynamic_slice_in_dim(summed, lax.axis_index("cuts") * portion, portion)
 

time: 164 us -> 300 us (1.83)
  waiting for transfers between devices: 29.3 us -> 251 us
  blocking collectives: 105 us -> 0 us
  other arithmetic: 6.78 us -> 25.7 us
    all_gather x0 -> x1, waiting for transfers between devices: none -> 222 us  [on_device(): summed = jnp.sum(lax.all_gather(partial_sum, ('cuts', 'stem')), axis=0)]
    psum x1 -> x0, blocking collectives: 105 us -> none  [on_device(): summed = lax.psum(partial_sum, ('cuts', 'stem'))]
    reduce_sum x0 -> x1, other arithmetic: none -> 18.9 us  [on_device(): summed = jnp.sum(lax.all_gather(partial_sum, ('cuts', 'stem')), axis=0)]
  transfers between devices with their start and end apart: 1 -> 2, of which waited for: 1 -> 2; matrix products, arithmetic and copies ran while one was open for 6% -> 3% of each run, Pallas kernels for 0% -> 0%
where the time goes in v3:
time: 300 us
  waiting for transfers between devices  251 us (84%)
  other arithmetic  25.7 us (9%)
  between operations  13.4 us (4%)
  matrix products  6.47 us (2%)
  local copies, waits for them, and re-layouts  3.52 us (1%)
    all_gather x1, waiting for transfers between devices, on_device(): summed = jnp.sum(lax.all_gather(partial_sum, ('cuts', 'stem')), axis=0)  222 us
    all_gather x1, waiting for transfers between devices, on_device(): fragment = lax.all_gather(stem_tensor, 'stem', axis=0, tiled=True)  28.5 us
    reduce_sum x1, other arithmetic, on_device(): summed = jnp.sum(lax.all_gather(partial_sum, ('cuts', 'stem')), axis=0)  18.9 us
  transfers between devices with their start and end apart: 2, of which 2 were waited for; matrix products, arithmetic and copies ran while one was open for 3% of the time, Pallas kernels for 0%

profile of v3, /device:TPU:1, one launch (start us, length us, event | category | flops | bytes accessed | tf_op | source)
XLA Modules:
  0.0 300.1 jit_solution(3428648421434726845)
XLA Ops:
  6.5 0.0 all-gather.4.cloned.1.call-start
  6.5 0.7 all-gather.4.cloned.1.call-update
  7.3 0.0 all-gather.6.cloned.1.call-start
  7.3 2.9 copy.9
  10.2 0.1 slice_negate_fusion.1
  10.3 0.0 copy-start.1
  10.3 2.3 maximum_maximum_fusion
  12.6 0.1 copy-done.1
  12.6 0.9 slice_negate_fusion
  13.5 3.5 %maximum_maximum_fusion.1 = bf16[8,16,128,128]{3,2,1,0:T(8,128)(2,1)} fusion(bf16[8,16,64,64]{3,2,1,0:T(8,128)(2,1)S(1)} %get-tuple-element.6, bf16[8,16,64,64]{3,2,1,0:T(8,128)(2,1)S(1)} %get-tuple-element.5, bf16[8,16,64,128]{3,2,1,0:T(8,128)(2,1)S(1)} %copy-done.1), kind=kLoop, calls=%fused_computation.1 | loop fusion | flops 12582912 | bytes 8388608 | tf_op jit(solution)/shard_map/concatenate | solution.py:13
  17.1 28.5 %all-gather.4.cloned.1.call-done = bf16[8,64,1024]{2,1,0:T(8,128)(2,1)} async-done(((bf16[2,64,1024]{2,1,0:T(8,128)(2,1)}), bf16[8,64,1024]{2,1,0:T(8,128)(2,1)}) %all-gather.4.cloned.1.call-update) | async-done | bytes 1048592 | tf_op jit(solution)/shard_map/all_gather | solution.py:20
  45.6 0.0 copy-start
  45.6 5.0 %convolution_convert_fusion = bf16[2048,512]{0,1:T(8,128)(2,1)S(1)} fusion(bf16[1024,2048]{0,1:T(8,128)(2,1)} %bitcast.17, bf16[512,1024]{1,0:T(8,128)(2,1)} %bitcast.19), kind=kOutput, calls=%fused_computation.2 | convolution fusion | flops 2148532224 | bytes 7340032 | tf_op jit(solution)/shard_map/dot_general | solution.py:22
  50.6 0.0 copy-done
  50.6 1.5 fusion
  52.0 0.0 all-gather.6.cloned.1.call-update
  52.1 221.6 %all-gather.6.cloned.1.call-done = f32[512,1,8192]{2,1,0:T(1,128)} async-done(((f32[1,1,8192]{2,1,0:T(1,128)}), f32[512,1,8192]{2,1,0:T(1,128)}) %all-gather.6.cloned.1.call-update) | async-done | bytes 16777232 | tf_op jit(solution)/shard_map/all_gather | solution.py:28
  273.7 18.9 %reduce_sum.9 = f32[8192]{0:T(1024)S(1)} reduce(f32[512,1,8192]{2,1,0:T(1,128)} %all-gather.6.cloned.1.call-done, f32[]{:T(128)} %constant.2.clone.1), dimensions={0,1}, to_apply=%region_0.0 | reduce | flops 4186112 | bytes 16809988 | tf_op jit(solution)/shard_map/reduce_sum | solution.py:28
  292.7 0.6 dynamic_slice.3
Async XLA Ops:
  6.5 39.0 %all-gather.4.cloned.1.call-start = ((), (), s32[]{:S(2)}) async-start(), calls=%async_computation | async-start | bytes 1310720 | tf_op jit(solution)/shard_map/all_gather | solution.py:20
  7.3 266.5 %all-gather.6.cloned.1.call-start = ((), (), s32[]{:S(2)}) async-start(), calls=%async_computation.1 | async-start | bytes 16809984 | tf_op jit(solution)/shard_map/all_gather | solution.py:28
  10.3 2.3 copy-start.1
  45.6 5.0 %copy-start = (bf16[8,16,128,128]{3,2,1,0:T(8,128)(2,1)S(1)}, bf16[8,16,128,128]{3,2,1,0:T(8,128)(2,1)}, u32[]{:S(2)}) copy-start(bf16[8,16,128,128]{3,2,1,0:T(8,128)(2,1)} %maximum_maximum_fusion.1) | copy-start | bytes 12582916
Sparse Core Ops, SparseCore 0:
  9.5 36.0 all-gather.3
  52.2 221.4 all-gather.5
